TPU v7x, 256 devices: a whole 4x4x8 slice. The times are simulated.
256 devices in a mesh: sub: 64 (over z, y, core), grp: 4 (over x).
Axes of the slice: x: 4, y: 4, z: 8, core: 2. Of those that a mesh axis runs over, the one named last changes fastest.
Arguments:
- coarse: float32 [6144, 128], P(('sub', 'grp')), may hold values from -6 to 6
- corner_idx: int32 [256, 24], P(('sub', 'grp')), may hold values from 0 to 6143, as said below
- coupling: bfloat16 [393216, 24], P(('sub', 'grp')), may hold values from -1.25 to 1.25
- force: bfloat16 [131072, 3, 128], P(('sub', 'grp')), may hold values from -6 to 6
- panel_inv: bfloat16 [1024, 384, 384], P(('sub', 'grp')), as said below
- panel_nodes: int32 [256, 4], P(('sub', 'grp')), may hold values from 64 to 128, as said below
- strain_disp: bfloat16 [6, 24, 32768], P(None, None, ('sub', 'grp')), may hold values from -1.25 to 1.25
- modulus: float32 [32768], P(('sub', 'grp')), may hold values from 0.5 to 4
- connect: int32 [8, 32768], P(None, ('sub', 'grp')), may hold values from 0 to 511, as said below
- interface: int32 [256, 224], P(('sub', 'grp')), may hold values from 0 to 511, as said below
- nodal_volume: float32 [131072], P(('sub', 'grp')), may hold values from 4 to 16
Outputs:
- displacement: bfloat16 [131072, 3, 128], P(('sub', 'grp'))
- nodal_stress: bfloat16 [131072, 6, 128], P(('sub', 'grp'))
Inputs may be any that keep to these rules, and one draw needn't show every extreme that they name: `corner_idx`: the rows of subdomain (s, g) lie in the coarse blocks of subdomains (s', g') with |s' - s| <= 1 that exist, including blocks of all grp indices; they come in triples of consecutive rows. `panel_nodes`: every subdomain has one panel with exactly 128 live nodes and one with 64. `connect`: every entry is a live node of its subdomain (slot j < panel_nodes of its panel). `interface`: each row holds 224 distinct live nodes as eight lists: sub-lo (64), sub-hi (64), grp-lo (32), grp-hi (32), then edges ll, lh, hl, hh (8 each; first letter the sub side, second the grp side). Entry k of a list of (s, g) is the same physical node as entry k of the facing list of each neighbour: sub-hi with sub-lo of (s + 1, g), grp-hi with grp-lo of (s, g + 1); edge (x, y) with the edge of the neighbour across it that has the opposite letter on each side crossed. `panel_inv`: given inverses of the padded panels.
All inputs are finite; a program needn't handle non-finite values.
Results may differ from a plain program's by a relative error of at most 0.0058.
Values sent between devices are 32-bit elements; how exact they have to be, the bound alone decides.
A program may use at most 64 MiB of HBM per device.

v0:
```python
import jax
import jax.numpy as jnp
from jax import lax
from jax.sharding import PartitionSpec as P

NIS = 64
NIG = 32
NED = 8
POISSON = 0.3


def padded(block, sides, width):
    for axis, dim in sides:
        count = lax.axis_size(axis)
        forward = [(i, i + 1) for i in range(count - 1)]
        backward = [(target, source) for source, target in forward]
        low = lax.ppermute(
            lax.slice_in_dim(block, block.shape[dim] - width, None, axis=dim), axis, forward
        )
        high = lax.ppermute(lax.slice_in_dim(block, 0, width, axis=dim), axis, backward)
        block = jnp.concatenate([low, block, high], axis=dim)
    return block


def iso_matrix():
    lame_first = POISSON / ((1.0 + POISSON) * (1.0 - 2.0 * POISSON))
    shear_mod = 0.5 / (1.0 + POISSON)
    upper_block = jnp.full((3, 3), lame_first, jnp.float32) + jnp.eye(3, dtype=jnp.float32) * (
        2.0 * shear_mod
    )
    shear_block = jnp.eye(3, dtype=jnp.float32) * shear_mod
    zero_block = jnp.zeros((3, 3), jnp.float32)
    return jnp.concatenate(
        [
            jnp.concatenate([upper_block, zero_block], 1),
            jnp.concatenate([zero_block, shear_block], 1),
        ],
        0,
    )


def shards(
    coarse,
    corner_idx,
    coupling,
    force,
    panel_inv,
    panel_nodes,
    strain_disp,
    modulus,
    connect,
    interface,
    nodal_volume,
):
    group_rows = lax.all_gather(coarse, "grp", axis=0, tiled=True)
    block_rows = group_rows.shape[0]
    nearby = padded(group_rows, (("sub", 0),), block_rows)
    offset = (lax.axis_index("sub") - 1) * block_rows
    local_rows = corner_idx[0] - offset
    selector = (local_rows[:, None] == jnp.arange(3 * block_rows, dtype=jnp.int32)[None, :]).astype(
        jnp.float32
    )
    corner_vals = jnp.dot(selector, nearby, precision=lax.Precision.HIGHEST)
    node_count = force.shape[0]
    load_cases = force.shape[2]
    panels = panel_inv.shape[0]
    panel_rows = panel_inv.shape[1]
    correction = jnp.dot(coupling.astype(jnp.float32), corner_vals, precision=lax.Precision.HIGHEST)
    live_mask = jnp.arange(panel_rows)[None, :] < 3 * panel_nodes[0][:, None]
    reduced = (force.reshape(3 * node_count, load_cases).astype(jnp.float32) - correction).reshape(
        panels, panel_rows, load_cases
    )
    reduced = jnp.where(live_mask[:, :, None], reduced, 0.0).astype(jnp.bfloat16)
    solved = jnp.einsum("prc,pcl->prl", panel_inv, reduced, preferred_element_type=jnp.float32)
    displaced = (
        jnp.where(live_mask[:, :, None], solved, 0.0)
        .astype(jnp.bfloat16)
        .reshape(node_count, 3 * load_cases)
    )
    elem_count = connect.shape[1]
    element = displaced[connect.T].reshape(elem_count, 24, load_cases)
    strain = jnp.einsum("ije,ejl->eil", strain_disp, element, preferred_element_type=jnp.float32)
    stress = (
        jnp.einsum("ik,ekl->eil", iso_matrix(), strain, precision=lax.Precision.HIGHEST)
        * modulus[:, None, None]
    )
    node_range = jnp.arange(node_count, dtype=jnp.int32)
    incidence = jnp.sum(
        (connect[:, None, :] == node_range[None, :, None]).astype(jnp.float32), axis=0
    )
    partial_value = jnp.dot(
        incidence, stress.reshape(elem_count, 6 * load_cases), precision=lax.Precision.HIGHEST
    ).reshape(node_count, 6, load_cases)
    node_ids = interface[0]
    picker = (node_ids[:, None] == node_range[None, :]).astype(jnp.float32)
    iface_rows = jnp.dot(
        picker, partial_value.reshape(node_count, 6 * load_cases), precision=lax.Precision.HIGHEST
    ).reshape(-1, 6, load_cases)
    start_edge = 2 * NIS + 2 * NIG
    faces_sub = iface_rows[: 2 * NIS].reshape(2, NIS, 6, load_cases)
    near_sub = padded(faces_sub, (("sub", 0),), 1)
    faces_sub = faces_sub + jnp.stack([near_sub[0], near_sub[3]])
    faces_grp = iface_rows[2 * NIS : start_edge].reshape(2, NIG, 6, load_cases)
    near_grp = padded(faces_grp, (("grp", 0),), 1)
    faces_grp = faces_grp + jnp.stack([near_grp[0], near_grp[3]])
    edge_block = iface_rows[start_edge:].reshape(2, 2, NED, 6, load_cases)
    beside_all = padded(edge_block, (("sub", 0), ("grp", 1)), 1)
    along_sub = jnp.stack([beside_all[0, 1:3], beside_all[3, 1:3]])
    along_grp = jnp.stack([beside_all[1:3, 0], beside_all[1:3, 3]], axis=1)
    diagonal = jnp.stack(
        [
            jnp.stack([beside_all[0, 0], beside_all[0, 3]]),
            jnp.stack([beside_all[3, 0], beside_all[3, 3]]),
        ]
    )
    edge_block = edge_block + along_sub + along_grp + diagonal
    summed_rows = jnp.concatenate(
        [
            faces_sub.reshape(-1, 6, load_cases),
            faces_grp.reshape(-1, 6, load_cases),
            edge_block.reshape(-1, 6, load_cases),
        ]
    )
    placed = jnp.dot(
        picker.T, summed_rows.reshape(-1, 6 * load_cases), precision=lax.Precision.HIGHEST
    ).reshape(node_count, 6, load_cases)
    on_face = jnp.sum(picker, axis=0) > 0.5
    summed = jnp.where(on_face[:, None, None], placed, partial_value)
    stress_out = (summed / nodal_volume[:, None, None]).astype(jnp.bfloat16)
    return (displaced.reshape(node_count, 3, load_cases), stress_out)


def solution(mesh):
    placed = (
        P(("sub", "grp"), None),
        P(("sub", "grp"), None),
        P(("sub", "grp"), None),
        P(("sub", "grp"), None, None),
        P(("sub", "grp"), None, None),
        P(("sub", "grp"), None),
        P(None, None, ("sub", "grp")),
        P(("sub", "grp")),
        P(None, ("sub", "grp")),
        P(("sub", "grp"), None),
        P(("sub", "grp")),
    )
    return jax.shard_map(
        shards,
        mesh=mesh,
        in_specs=placed,
        out_specs=(P(("sub", "grp"), None, None), P(("sub", "grp"), None, None)),
        check_vma=False,
    )
```

profile of v0, /device:TPU:123, one launch (start us, length us, event | category | flops | bytes accessed | tf_op | source)
XLA Modules:
  0.0 98.0 jit_solution(14922059316060356889)
XLA Ops:
  0.6 9.4 %all_gather.3 = f32[96,128]{1,0:T(8,128)S(1)} all-gather(f32[24,128]{1,0:T(8,128)} %param.11), channel_id=1, replica_groups=mesh['sub'=64,'grp'=4] {'grp'}, dimensions={0}, use_global_device_ids=true | all-gather | bytes 61440 | tf_op jit(solution)/shard_map/all_gather | solution.py:55
  10.1 5.5 %collective-permute-start.1 = (f32[96,128]{1,0:T(8,128)S(1)}, f32[96,128]{1,0:T(8,128)S(1)}, u32[]{:S(2)}, u32[]{:S(2)}) collective-permute-start(f32[96,128]{1,0:T(8,128)S(1)} %all_gather.3), channel_id=1, source_target_pairs={{4,0},{8,4},{12,8},{16,12},{20,16},{24,20},{28,24},{32,28},{36,32}... | collective-permute-start | bytes 147464 | tf_op jit(solution)/shard_map/ppermute | solution.py:20
  15.5 4.3 %collective-permute-start = (f32[96,128]{1,0:T(8,128)S(1)}, f32[96,128]{1,0:T(8,128)S(1)}, u32[]{:S(2)}, u32[]{:S(2)}) collective-permute-start(f32[96,128]{1,0:T(8,128)S(1)} %all_gather.3), channel_id=1, source_target_pairs={{0,4},{4,8},{8,12},{12,16},{16,20},{20,24},{24,28},{28,32},{32,36}... | collective-permute-start | bytes 147464 | tf_op jit(solution)/shard_map/ppermute | solution.py:17
  19.9 0.7 compare_select_fusion
  20.6 1.6 %convert_reduce_fusion = f32[512,128]{1,0:T(8,128)} fusion(s32[8,128]{1,0:T(8,128)} %param.19), kind=kLoop, calls=%fused_computation.3 | loop fusion | flops 1507328 | bytes 266240 | tf_op jit(solution)/shard_map/reduce_sum | solution.py:88
  22.2 0.7 multiply_bitcast_fusion
  23.1 0.7 subtract_bitcast_fusion
  23.8 1.6 %copy.35 = bf16[6,24,128]{1,0,2:T(8,128)(2,1)} copy(bf16[6,24,128]{2,1,0:T(8,128)(2,1)} %param.17) | data formatting | bytes 73728 | tf_op args[6]
  25.4 1.3 %copy.29 = f32[512,3,128]{2,1,0:T(4,128)S(1)} copy(bf16[512,3,128]{2,0,1:T(8,128)(2,1)} %param.14) | data formatting | bytes 1179648 | tf_op jit(solution)/shard_map/convert_element_type | solution.py:70
  26.8 1.2 %reshape.111 = f32[1536,128]{1,0:T(8,128)} reshape(f32[512,3,128]{2,1,0:T(4,128)S(1)} %copy.29) | data formatting | bytes 1572864 | tf_op jit(solution)/shard_map/convert_element_type | solution.py:70
  28.0 1.4 %copy.30 = f32[1536,128]{0,1:T(8,128)S(1)} copy(f32[1536,128]{1,0:T(8,128)} %reshape.111) | data formatting | bytes 1572864 | tf_op jit(solution)/shard_map/convert_element_type | solution.py:70
  29.4 0.2 fusion.14
  29.7 0.5 fusion
  30.2 0.5 fusion.3
  30.7 0.2 copy.32
  31.0 0.2 reshape.106
  31.1 3.9 %gather_fusion = bf16[1024,384]{1,0:T(8,128)(2,1)S(1)} fusion(bf16[512,384]{1,0:T(8,128)(2,1)S(1)} %reshape.106, s32[1024]{0:T(1024)S(1)} %broadcast_clamp_fusion), kind=kCustom, calls=%fused_computation | custom fusion | bytes 1576960 | tf_op jit(solution)/shard_map/gather | solution.py:81
  35.1 0.4 reshape.107
  35.5 1.3 %convolution_bitcast_fusion.1 = f32[128,6,128]{2,1,0:T(8,128)S(1)} fusion(bf16[128,24,128]{2,1,0:T(8,128)(2,1)S(1)} %reshape.107, bf16[6,24,128]{1,0,2:T(8,128)(2,1)} %copy.35), kind=kOutput, calls=%fused_computation.10 | convolution fusion | flops 4718592 | bytes 1216512 | tf_op jit(solution)/shard_map/ije,ejl->eil/dot_general | solution.py:82
  36.8 0.7 fusion.2
  37.4 0.2 copy.36
  37.6 2.3 %fusion.37 = f32[512,768]{1,0:T(8,128)S(1)} fusion(f32[512,128]{1,0:T(8,128)} %convert_reduce_fusion, f32[128,768]{0,1:T(8,128)S(1)} %bitcast.76), kind=kOutput, calls=%fused_computation.75 | convolution fusion | flops 603979776 | bytes 2228224 | tf_op jit(solution)/shard_map/dot_general | solution.py:91
  40.0 1.0 fusion.6
  41.0 2.4 %collective-permute-start.6 = (f32[1,2,8,6,128]{4,2,3,1,0:T(8,128)S(1)}, f32[1,2,8,6,128]{4,2,3,1,0:T(8,128)S(1)}, u32[]{:S(2)}, u32[]{:S(2)}) collective-permute-start(f32[1,2,8,6,128]{4,2,3,1,0:T(8,128)S(1)} %get-tuple-element.12), channel_id=1, source_target_pairs={{0,4},{4,8},{8,12},{12,16},{16,20},{20,24},{24,28},{28,32},{32,36}... | collective-permute-start | bytes 147464 | tf_op jit(solution)/shard_map/ppermute | solution.py:17
  43.4 1.9 %collective-permute-start.7 = (f32[1,2,8,6,128]{4,2,3,1,0:T(8,128)S(1)}, f32[1,2,8,6,128]{4,2,3,1,0:T(8,128)S(1)}, u32[]{:S(2)}, u32[]{:S(2)}) collective-permute-start(f32[1,2,8,6,128]{4,2,3,1,0:T(8,128)S(1)} %get-tuple-element.13), channel_id=1, source_target_pairs={{4,0},{8,4},{12,8},{16,12},{20,16},{24,20},{28,24},{32,28},{36,32}... | collective-permute-start | bytes 147464 | tf_op jit(solution)/shard_map/ppermute | solution.py:20
  45.3 6.8 %collective-permute-done.7 = f32[1,2,8,6,128]{4,2,3,1,0:T(8,128)S(1)} collective-permute-done((f32[1,2,8,6,128]{4,2,3,1,0:T(8,128)S(1)}, f32[1,2,8,6,128]{4,2,3,1,0:T(8,128)S(1)}, u32[]{:S(2)}, u32[]{:S(2)}) %collective-permute-start.7) | collective-permute-done | bytes 49184 | tf_op jit(solution)/shard_map/ppermute | solution.py:20
  52.2 1.9 %collective-permute-start.8 = (f32[4,1,8,6,128]{4,2,3,1,0:T(8,128)S(1)}, f32[4,1,8,6,128]{4,2,3,1,0:T(8,128)S(1)}, u32[]{:S(2)}, u32[]{:S(2)}) collective-permute-start(f32[4,1,8,6,128]{4,2,3,1,0:T(8,128)S(1)} %get-tuple-element.14), channel_id=1, source_target_pairs={{0,1},{1,2},{2,3},{4,5},{5,6},{6,7},{8,9},{9,10},{10,11},{12,13},{... | collective-permute-start | bytes 294920 | tf_op jit(solution)/shard_map/ppermute | solution.py:17
  54.1 3.4 %collective-permute-start.9 = (f32[4,1,8,6,128]{4,2,3,1,0:T(8,128)S(1)}, f32[4,1,8,6,128]{4,2,3,1,0:T(8,128)S(1)}, u32[]{:S(2)}, u32[]{:S(2)}) collective-permute-start(f32[4,1,8,6,128]{4,2,3,1,0:T(8,128)S(1)} %get-tuple-element.15), channel_id=1, source_target_pairs={{1,0},{2,1},{3,2},{5,4},{6,5},{7,6},{9,8},{10,9},{11,10},{13,12},{... | collective-permute-start | bytes 294920 | tf_op jit(solution)/shard_map/ppermute | solution.py:20
  57.5 2.5 %collective-permute-done.9 = f32[4,1,8,6,128]{4,2,3,1,0:T(8,128)S(1)} collective-permute-done((f32[4,1,8,6,128]{4,2,3,1,0:T(8,128)S(1)}, f32[4,1,8,6,128]{4,2,3,1,0:T(8,128)S(1)}, u32[]{:S(2)}, u32[]{:S(2)}) %collective-permute-start.9) | collective-permute-done | bytes 98336 | tf_op jit(solution)/shard_map/ppermute | solution.py:20
  60.1 0.7 fusion.35
  60.8 1.6 %slice.85 = f32[1,32,6,128]{3,2,1,0:T(8,128)} reshape(f32[32,768]{1,0:T(8,128)} %get-tuple-element.9) | data formatting | bytes 196608 | tf_op jit(solution)/shard_map/slice | solution.py:18
  62.4 0.7 slice.87
  63.1 2.7 %collective-permute-start.5 = (f32[1,32,6,128]{3,2,1,0:T(8,128)}, f32[1,32,6,128]{3,2,1,0:T(8,128)S(1)}, u32[]{:S(2)}, u32[]{:S(2)}) collective-permute-start(f32[1,32,6,128]{3,2,1,0:T(8,128)} %slice.87), channel_id=1, source_target_pairs={{1,0},{2,1},{3,2},{5,4},{6,5},{7,6},{9,8},{10,9},{11,10},{13,12},{... | collective-permute-start | bytes 294920 | tf_op jit(solution)/shard_map/ppermute | solution.py:20
  65.8 2.5 %collective-permute-start.4 = (f32[1,32,6,128]{3,2,1,0:T(8,128)}, f32[1,32,6,128]{3,2,1,0:T(8,128)S(1)}, u32[]{:S(2)}, u32[]{:S(2)}) collective-permute-start(f32[1,32,6,128]{3,2,1,0:T(8,128)} %slice.85), channel_id=1, source_target_pairs={{0,1},{1,2},{2,3},{4,5},{5,6},{6,7},{8,9},{9,10},{10,11},{12,13},{... | collective-permute-start | bytes 294920 | tf_op jit(solution)/shard_map/ppermute | solution.py:17
  68.5 0.7 collective-permute-done.5
  69.2 2.6 %collective-permute-done.4 = f32[1,32,6,128]{3,2,1,0:T(8,128)S(1)} collective-permute-done((f32[1,32,6,128]{3,2,1,0:T(8,128)}, f32[1,32,6,128]{3,2,1,0:T(8,128)S(1)}, u32[]{:S(2)}, u32[]{:S(2)}) %collective-permute-start.4) | collective-permute-done | bytes 98336 | tf_op jit(solution)/shard_map/ppermute | solution.py:17
  71.8 0.9 fusion.34
  72.6 1.7 %slice.80 = f32[1,64,6,128]{3,2,1,0:T(8,128)} reshape(f32[64,768]{1,0:T(8,128)} %get-tuple-element.6) | data formatting | bytes 393216 | tf_op jit(solution)/shard_map/slice | solution.py:18
  74.3 1.7 %slice.82 = f32[1,64,6,128]{3,2,1,0:T(8,128)} reshape(f32[64,768]{1,0:T(8,128)} %get-tuple-element.8) | data formatting | bytes 393216 | tf_op jit(solution)/shard_map/slice | solution.py:20
  76.0 1.9 %collective-permute-start.3 = (f32[1,64,6,128]{3,2,1,0:T(8,128)}, f32[1,64,6,128]{3,2,1,0:T(8,128)}, u32[]{:S(2)}, u32[]{:S(2)}) collective-permute-start(f32[1,64,6,128]{3,2,1,0:T(8,128)} %slice.82), channel_id=1, source_target_pairs={{4,0},{8,4},{12,8},{16,12},{20,16},{24,20},{28,24},{32,28},{36,32}... | collective-permute-start | bytes 589832 | tf_op jit(solution)/shard_map/ppermute | solution.py:20
  77.9 7.0 %collective-permute-start.2 = (f32[1,64,6,128]{3,2,1,0:T(8,128)}, f32[1,64,6,128]{3,2,1,0:T(8,128)}, u32[]{:S(2)}, u32[]{:S(2)}) collective-permute-start(f32[1,64,6,128]{3,2,1,0:T(8,128)} %slice.80), channel_id=1, source_target_pairs={{0,4},{4,8},{8,12},{12,16},{16,20},{20,24},{24,28},{28,32},{32,36}... | collective-permute-start | bytes 589832 | tf_op jit(solution)/shard_map/ppermute | solution.py:17
  84.9 2.1 %reshape_reshape.3 = bf16[512,3,128]{2,1,0:T(4,128)(2,1)} reshape(bf16[4,384,128]{2,1,0:T(8,128)(2,1)} %copy-done.1) | data formatting | bytes 786432 | tf_op jit(solution)/shard_map/reshape;reshape | solution.py:130
  87.0 1.6 %copy.39 = f32[512,768]{0,1:T(8,128)} copy(f32[512,768]{1,0:T(8,128)S(1)} %fusion.37) | data formatting | bytes 3145728 | tf_op jit(solution)/shard_map/dot_general | solution.py:91
  88.6 1.8 %copy.41 = bf16[512,3,128]{2,0,1:T(8,128)(2,1)} copy(bf16[512,3,128]{2,1,0:T(4,128)(2,1)} %reshape_reshape.3) | data formatting | bytes 786432
  90.5 1.9 %copy.40 = f32[512,6,128]{2,0,1:T(8,128)S(1)} copy(f32[512,6,128]{0,2,1:T(8,128)} %bitcast.74) | data formatting | bytes 3145728 | tf_op jit(solution)/shard_map/reshape | solution.py:93
  92.4 1.1 %pad_maximum_fusion = f32[2,64,6,128]{3,2,1,0:T(8,128)S(1)} fusion(f32[1,64,6,128]{3,2,1,0:T(8,128)} %collective-permute-done.3, f32[1,64,6,128]{3,2,1,0:T(8,128)} %collective-permute-done.2), kind=kLoop, calls=%fused_computation.15 | loop fusion | flops 98304 | bytes 786432 | tf_op jit(solution)/shard_map/stack | solution.py:102
  93.7 1.2 %copy.37 = f32[768,224]{1,0:T(8,128)} copy(f32[768,224]{0,1:T(8,128)S(1)} %maximum_bitcast_fusion) | data formatting | bytes 1376256 | tf_op jit(solution)/shard_map/dot_general | solution.py:124
  94.9 3.2 %divide_convert_fusion = bf16[512,6,128]{2,0,1:T(8,128)(2,1)} fusion(f32[512,6,128]{2,0,1:T(8,128)S(1)} %copy.40, f32[6,128,224]{2,1,0:T(8,128)} %bitcast.78, f32[512]{0:T(512)S(1)} %copy-done.7, pred[512]{0:T(512)(128)(4,1)S(1)} %broadcast_compare_fusion, s32[224]{0:T(256)S(1)} %bitcast.86), kind=kOutput, calls=%fused_computation.5 | convolution fusion | flops 1058373632 | bytes 3050880 | tf_op jit(solution)/shard_map/dot_general | solution.py:124
  (45 shorter events, 0.8 us)
Async XLA Ops:
  0.6 29.6 %copy-start = (bf16[4,384,384]{2,1,0:T(8,128)(2,1)S(1)}, bf16[4,384,384]{2,1,0:T(8,128)(2,1)}, u32[]{:S(2)}) copy-start(bf16[4,384,384]{2,1,0:T(8,128)(2,1)} %param.15) | copy-start | bytes 3538948
  10.1 19.3 %collective-permute-start.1 = (f32[96,128]{1,0:T(8,128)S(1)}, f32[96,128]{1,0:T(8,128)S(1)}, u32[]{:S(2)}, u32[]{:S(2)}) collective-permute-start(f32[96,128]{1,0:T(8,128)S(1)} %all_gather.3), channel_id=1, source_target_pairs={{4,0},{8,4},{12,8},{16,12},{20,16},{24,20},{28,24},{32,28},{36,32}... | collective-permute-start | bytes 147464 | tf_op jit(solution)/shard_map/ppermute | solution.py:20
  15.5 13.9 %collective-permute-start = (f32[96,128]{1,0:T(8,128)S(1)}, f32[96,128]{1,0:T(8,128)S(1)}, u32[]{:S(2)}, u32[]{:S(2)}) collective-permute-start(f32[96,128]{1,0:T(8,128)S(1)} %all_gather.3), channel_id=1, source_target_pairs={{0,4},{4,8},{8,12},{12,16},{16,20},{20,24},{24,28},{28,32},{32,36}... | collective-permute-start | bytes 147464 | tf_op jit(solution)/shard_map/ppermute | solution.py:17
  26.8 2.9 %copy-start.4 = (bf16[1536,24]{0,1:T(8,128)(2,1)S(1)}, bf16[1536,24]{0,1:T(8,128)(2,1)}, u32[]{:S(2)}) copy-start(bf16[1536,24]{0,1:T(8,128)(2,1)} %param.13) | copy-start | bytes 221188
  30.9 4.1 %copy-start.1 = (bf16[4,384,128]{2,1,0:T(8,128)(2,1)}, bf16[4,384,128]{2,1,0:T(8,128)(2,1)S(1)}, u32[]{:S(2)}) copy-start(bf16[4,384,128]{2,1,0:T(8,128)(2,1)S(1)} %copy.32) | copy-start | bytes 1179652
  35.1 1.7 %copy-start.6 = (f32[128]{0:T(128)S(1)}, f32[128]{0:T(128)}, u32[]{:S(2)}) copy-start(f32[128]{0:T(128)} %param.18) | copy-start | bytes 1540
  37.4 2.6 %copy-start.5 = (s32[1,224]{1,0:T(1,128)S(1)}, s32[1,224]{1,0:T(1,128)}, u32[]{:S(2)}) copy-start(s32[1,224]{1,0:T(1,128)} %param.20) | copy-start | bytes 2692
  41.0 4.4 %collective-permute-start.6 = (f32[1,2,8,6,128]{4,2,3,1,0:T(8,128)S(1)}, f32[1,2,8,6,128]{4,2,3,1,0:T(8,128)S(1)}, u32[]{:S(2)}, u32[]{:S(2)}) collective-permute-start(f32[1,2,8,6,128]{4,2,3,1,0:T(8,128)S(1)} %get-tuple-element.12), channel_id=1, source_target_pairs={{0,4},{4,8},{8,12},{12,16},{16,20},{20,24},{24,28},{28,32},{32,36}... | collective-permute-start | bytes 147464 | tf_op jit(solution)/shard_map/ppermute | solution.py:17
  43.4 8.7 %collective-permute-start.7 = (f32[1,2,8,6,128]{4,2,3,1,0:T(8,128)S(1)}, f32[1,2,8,6,128]{4,2,3,1,0:T(8,128)S(1)}, u32[]{:S(2)}, u32[]{:S(2)}) collective-permute-start(f32[1,2,8,6,128]{4,2,3,1,0:T(8,128)S(1)} %get-tuple-element.13), channel_id=1, source_target_pairs={{4,0},{8,4},{12,8},{16,12},{20,16},{24,20},{28,24},{32,28},{36,32}... | collective-permute-start | bytes 147464 | tf_op jit(solution)/shard_map/ppermute | solution.py:20
  52.2 5.4 %collective-permute-start.8 = (f32[4,1,8,6,128]{4,2,3,1,0:T(8,128)S(1)}, f32[4,1,8,6,128]{4,2,3,1,0:T(8,128)S(1)}, u32[]{:S(2)}, u32[]{:S(2)}) collective-permute-start(f32[4,1,8,6,128]{4,2,3,1,0:T(8,128)S(1)} %get-tuple-element.14), channel_id=1, source_target_pairs={{0,1},{1,2},{2,3},{4,5},{5,6},{6,7},{8,9},{9,10},{10,11},{12,13},{... | collective-permute-start | bytes 294920 | tf_op jit(solution)/shard_map/ppermute | solution.py:17
  54.1 6.0 %collective-permute-start.9 = (f32[4,1,8,6,128]{4,2,3,1,0:T(8,128)S(1)}, f32[4,1,8,6,128]{4,2,3,1,0:T(8,128)S(1)}, u32[]{:S(2)}, u32[]{:S(2)}) collective-permute-start(f32[4,1,8,6,128]{4,2,3,1,0:T(8,128)S(1)} %get-tuple-element.15), channel_id=1, source_target_pairs={{1,0},{2,1},{3,2},{5,4},{6,5},{7,6},{9,8},{10,9},{11,10},{13,12},{... | collective-permute-start | bytes 294920 | tf_op jit(solution)/shard_map/ppermute | solution.py:20
  63.1 6.1 %collective-permute-start.5 = (f32[1,32,6,128]{3,2,1,0:T(8,128)}, f32[1,32,6,128]{3,2,1,0:T(8,128)S(1)}, u32[]{:S(2)}, u32[]{:S(2)}) collective-permute-start(f32[1,32,6,128]{3,2,1,0:T(8,128)} %slice.87), channel_id=1, source_target_pairs={{1,0},{2,1},{3,2},{5,4},{6,5},{7,6},{9,8},{10,9},{11,10},{13,12},{... | collective-permute-start | bytes 294920 | tf_op jit(solution)/shard_map/ppermute | solution.py:20
  65.8 5.9 %collective-permute-start.4 = (f32[1,32,6,128]{3,2,1,0:T(8,128)}, f32[1,32,6,128]{3,2,1,0:T(8,128)S(1)}, u32[]{:S(2)}, u32[]{:S(2)}) collective-permute-start(f32[1,32,6,128]{3,2,1,0:T(8,128)} %slice.85), channel_id=1, source_target_pairs={{0,1},{1,2},{2,3},{4,5},{5,6},{6,7},{8,9},{9,10},{10,11},{12,13},{... | collective-permute-start | bytes 294920 | tf_op jit(solution)/shard_map/ppermute | solution.py:17
  76.0 16.4 %collective-permute-start.3 = (f32[1,64,6,128]{3,2,1,0:T(8,128)}, f32[1,64,6,128]{3,2,1,0:T(8,128)}, u32[]{:S(2)}, u32[]{:S(2)}) collective-permute-start(f32[1,64,6,128]{3,2,1,0:T(8,128)} %slice.82), channel_id=1, source_target_pairs={{4,0},{8,4},{12,8},{16,12},{20,16},{24,20},{28,24},{32,28},{36,32}... | collective-permute-start | bytes 589832 | tf_op jit(solution)/shard_map/ppermute | solution.py:20
  77.9 14.5 %collective-permute-start.2 = (f32[1,64,6,128]{3,2,1,0:T(8,128)}, f32[1,64,6,128]{3,2,1,0:T(8,128)}, u32[]{:S(2)}, u32[]{:S(2)}) collective-permute-start(f32[1,64,6,128]{3,2,1,0:T(8,128)} %slice.80), channel_id=1, source_target_pairs={{0,4},{4,8},{8,12},{12,16},{16,20},{20,24},{24,28},{28,32},{32,36}... | collective-permute-start | bytes 589832 | tf_op jit(solution)/shard_map/ppermute | solution.py:17
  92.3 1.3 %copy-start.2 = (f32[64,768]{1,0:T(8,128)S(1)}, f32[64,768]{1,0:T(8,128)}, u32[]{:S(2)}) copy-start(f32[64,768]{1,0:T(8,128)} %get-tuple-element.7) | copy-start | bytes 589828
  92.3 1.3 %copy-start.3 = (f32[32,768]{1,0:T(8,128)S(1)}, f32[32,768]{1,0:T(8,128)}, u32[]{:S(2)}) copy-start(f32[32,768]{1,0:T(8,128)} %get-tuple-element.10) | copy-start | bytes 294916
  93.6 1.2 %copy-start.7 = (f32[512]{0:T(512)S(1)}, f32[512]{0:T(512)}, u32[]{:S(2)}) copy-start(f32[512]{0:T(512)} %param.21) | copy-start | bytes 6148
where the time goes:
time: 98.9 us; the launch traced here: 98 us
  starting transfers between devices  33.5 us (34%)
  local copies, waits for them, and re-layouts  24.9 us (25%)
  waiting for transfers between devices  12.6 us (13%)
  matrix products  9.65 us (10%)
  blocking collectives  9.42 us (10%)
  other arithmetic  6.77 us (7%)
  between operations  1.1 us (1%)
    ppermute x5, starting transfers between devices, padded(): lax.ppermute(lax.slice_in_dim(block, block.shape[dim] - width, None, axis...  18.1 us
    ppermute x5, starting transfers between devices, padded(): lax.ppermute(lax.slice_in_dim(block, 0, width, axis=dim), axis, backward)  15.4 us
    ppermute x5, waiting for transfers between devices, padded(): lax.ppermute(lax.slice_in_dim(block, 0, width, axis=dim), axis, backward)  9.97 us
    all_gather x1, blocking collectives, shards(): group_rows = lax.all_gather(coarse, 'grp', axis=0, tiled=True)  9.42 us
    convert_element_type x3, local copies, waits for them, and re-layouts, shards(): force.reshape(3 * node_count, load_cases).astype(jnp.float32) - correction  3.97 us
    gather x1, local copies, waits for them, and re-layouts, shards(): element = displaced[connect.T].reshape(elem_count, 24, load_cases)  3.92 us
    unnamed x18, local copies, waits for them, and re-layouts  3.52 us
    slice x4, local copies, waits for them, and re-layouts, padded(): lax.slice_in_dim(block, block.shape[dim] - width, None, axis=dim)  3.25 us
  transfers between devices with their start and end apart: 10, of which 4 were waited for; matrix products, arithmetic and copies ran while one was open for 17% of the time, Pallas kernels for 0%

commit v1 on v0

--- a/solution.py
+++ b/solution.py
@@ -7,6 +7,19 @@
 NIG = 32
 NED = 8
 POISSON = 0.3
+
+
+def ring_gather(value, axis, dim):
+    ways = lax.axis_size(axis)
+    up = [(d, (d + 1) % ways) for d in range(ways)]
+    down = [(d, (d - 1) % ways) for d in range(ways)]
+    earlier, later = ([value], [value])
+    for _ in range(ways // 2):
+        earlier.append(lax.ppermute(earlier[-1], axis, up))
+    for _ in range((ways - 1) // 2):
+        later.append(lax.ppermute(later[-1], axis, down))
+    line = jnp.concatenate([*earlier[::-1], *later[1:]], axis=dim)
+    return jnp.roll(line, (lax.axis_index(axis) - ways // 2) * value.shape[dim], axis=dim)
 
 
 def padded(block, sides, width):
@@ -52,7 +65,7 @@
     interface,
     nodal_volume,
 ):
-    group_rows = lax.all_gather(coarse, "grp", axis=0, tiled=True)
+    group_rows = ring_gather(coarse, "grp", 0)
     block_rows = group_rows.shape[0]
     nearby = padded(group_rows, (("sub", 0),), block_rows)
     offset = (lax.axis_index("sub") - 1) * block_rows

time: 98.9 us -> 93.9 us (0.949)
  blocking collectives: 9.42 us -> 0 us
  starting transfers between devices: 33.5 us -> 39.2 us
    all_gather x1 -> x0, blocking collectives: 9.42 us -> none  [shards(): group_rows = lax.all_gather(coarse, 'grp', axis=0, tiled=True)]
    ppermute x5, starting transfers between devices: 18.1 us -> 23.1 us  [padded(): lax.ppermute(lax.slice_in_dim(block, block.shape[dim] - width, None, axis...]
    ppermute x0 -> x3, starting transfers between devices: none -> 2.75 us  [the longest x2 2.5 us: ring_gather(): earlier.append(lax.ppermute(earlier[-1], axis, up))]
    ppermute x5, starting transfers between devices: 15.4 us -> 13.3 us  [padded(): lax.ppermute(lax.slice_in_dim(block, 0, width, axis=dim), axis, backward)]
    convert_element_type x3, local copies, waits for them, and re-layouts: 3.97 us -> 1.96 us  [shards(): force.reshape(3 * node_count, load_cases).astype(jnp.float32) - correction]
    unnamed x18 -> x25, local copies, waits for them, and re-layouts: 3.52 us -> 4.28 us
  transfers between devices with their start and end apart: 10 -> 13, of which waited for: 4 -> 4; matrix products, arithmetic and copies ran while one was open for 17% -> 16% of each run, Pallas kernels for 0% -> 0%
where the time goes in v1:
time: 93.9 us; the launch traced here: 93 us
  starting transfers between devices  39.2 us (42%)
  local copies, waits for them, and re-layouts  24.4 us (26%)
  waiting for transfers between devices  12.6 us (13%)
  matrix products  8.83 us (9%)
  other arithmetic  6.78 us (7%)
  between operations  1.12 us (1%)
    ppermute x5, starting transfers between devices, padded(): lax.ppermute(lax.slice_in_dim(block, block.shape[dim] - width, None, axis...  23.1 us
    ppermute x5, starting transfers between devices, padded(): lax.ppermute(lax.slice_in_dim(block, 0, width, axis=dim), axis, backward)  13.3 us
    ppermute x5, waiting for transfers between devices, padded(): lax.ppermute(lax.slice_in_dim(block, 0, width, axis=dim), axis, backward)  9.81 us
    unnamed x25, local copies, waits for them, and re-layouts  4.28 us
    gather x1, local copies, waits for them, and re-layouts, shards(): element = displaced[connect.T].reshape(elem_count, 24, load_cases)  3.92 us
    slice x4, local copies, waits for them, and re-layouts, padded(): lax.slice_in_dim(block, block.shape[dim] - width, None, axis=dim)  3.24 us
    dot_general x1, matrix products, shards(): jnp.dot(picker.T, summed_rows.reshape(-1, 6 * load_cases), precision=lax....  3.18 us
    ppermute x5, waiting for transfers between devices, padded(): lax.ppermute(lax.slice_in_dim(block, block.shape[dim] - width, None, axis...  2.81 us
  transfers between devices with their start and end apart: 13, of which 4 were waited for; matrix products, arithmetic and copies ran while one was open for 16% of the time, Pallas kernels for 0%

profile of v1, /device:TPU:123, one launch (start us, length us, event | category | flops | bytes accessed | tf_op | source)
XLA Modules:
  0.0 93.0 jit_solution(7339419901326776894)
XLA Ops:
  0.6 1.3 %collective-permute-start = (f32[24,128]{1,0:T(8,128)}, f32[24,128]{1,0:T(8,128)S(1)}, u32[]{:S(2)}, u32[]{:S(2)}) collective-permute-start(f32[24,128]{1,0:T(8,128)} %param.11), channel_id=1, source_target_pairs={{0,1},{1,2},{2,3},{3,0},{4,5},{5,6},{6,7},{7,4},{8,9},{9,10},{10,1... | collective-permute-start | bytes 36872 | tf_op jit(solution)/shard_map/ppermute | solution.py:18
  2.2 0.7 multiply_bitcast_fusion
  2.9 0.7 compare_select_fusion
  3.8 0.7 subtract_bitcast_fusion
  4.5 1.2 %collective-permute-start.1 = (f32[24,128]{1,0:T(8,128)S(1)}, f32[24,128]{1,0:T(8,128)S(1)}, u32[]{:S(2)}, u32[]{:S(2)}) collective-permute-start(f32[24,128]{1,0:T(8,128)S(1)} %collective-permute-done), channel_id=1, source_target_pairs={{0,1},{1,2},{2,3},{3,0},{4,5},{5,6},{6,7},{7,4},{8,9},{9,10},{10,1... | collective-permute-start | bytes 36872 | tf_op jit(solution)/shard_map/ppermute | solution.py:18
  5.7 1.6 %convert_reduce_fusion = f32[512,128]{1,0:T(8,128)} fusion(s32[8,128]{1,0:T(8,128)} %param.19), kind=kLoop, calls=%fused_computation.3 | loop fusion | flops 1507328 | bytes 266240 | tf_op jit(solution)/shard_map/reduce_sum | solution.py:101
  7.3 0.7 constant_dynamic-update-slice_fusion.5
  8.1 0.7 constant_dynamic-update-slice_fusion.1
  8.8 4.0 %collective-permute-start.4 = (f32[96,128]{1,0:T(8,128)S(1)}, f32[96,128]{1,0:T(8,128)S(1)}, u32[]{:S(2)}, u32[]{:S(2)}) collective-permute-start(f32[96,128]{1,0:T(8,128)S(1)} %constant_dynamic-slice_fusion), channel_id=1, source_target_pairs={{4,0},{8,4},{12,8},{16,12},{20,16},{24,20},{28,24},{32,28},{36,32}... | collective-permute-start | bytes 147464 | tf_op jit(solution)/shard_map/ppermute | solution.py:33
  12.8 4.9 %collective-permute-start.3 = (f32[96,128]{1,0:T(8,128)S(1)}, f32[96,128]{1,0:T(8,128)S(1)}, u32[]{:S(2)}, u32[]{:S(2)}) collective-permute-start(f32[96,128]{1,0:T(8,128)S(1)} %constant_dynamic-slice_fusion), channel_id=1, source_target_pairs={{0,4},{4,8},{8,12},{12,16},{16,20},{20,24},{24,28},{28,32},{32,36}... | collective-permute-start | bytes 147464 | tf_op jit(solution)/shard_map/ppermute | solution.py:30
  17.7 1.0 %copy.35 = bf16[6,24,128]{1,0,2:T(8,128)(2,1)S(1)} copy(bf16[6,24,128]{2,1,0:T(8,128)(2,1)} %param.17) | data formatting | bytes 73728 | tf_op args[6]
  18.7 1.3 %copy.29 = f32[512,3,128]{2,1,0:T(4,128)S(1)} copy(bf16[512,3,128]{2,0,1:T(8,128)(2,1)} %param.14) | data formatting | bytes 1179648 | tf_op jit(solution)/shard_map/convert_element_type | solution.py:83
  20.0 0.4 reshape.111
  20.4 0.3 copy.30
  20.9 0.5 fusion
  21.4 0.5 fusion.3
  22.4 3.9 %gather_fusion = bf16[1024,384]{1,0:T(8,128)(2,1)S(1)} fusion(bf16[512,384]{1,0:T(8,128)(2,1)S(1)} %reshape.106, s32[1024]{0:T(1024)S(1)} %broadcast_clamp_fusion), kind=kCustom, calls=%fused_computation | custom fusion | bytes 1576960 | tf_op jit(solution)/shard_map/gather | solution.py:94
  26.3 0.4 reshape.107
  26.7 0.4 convolution_bitcast_fusion.1
  27.1 0.6 fusion.2
  27.7 1.0 %copy.36 = f32[128,6,128]{0,2,1:T(8,128)} copy(f32[128,6,128]{2,1,0:T(8,128)S(1)} %fusion.2) | data formatting | bytes 786432 | tf_op jit(solution)/shard_map/mul | solution.py:97
  28.7 2.5 %fusion.37 = f32[512,768]{1,0:T(8,128)S(1)} fusion(f32[512,128]{1,0:T(8,128)} %convert_reduce_fusion, f32[128,768]{0,1:T(8,128)} %bitcast.76), kind=kOutput, calls=%fused_computation.84 | convolution fusion | flops 603979776 | bytes 2228224 | tf_op jit(solution)/shard_map/dot_general | solution.py:104
  31.2 0.9 %fusion.6 = f32[224,768]{1,0:T(8,128)S(1)} fusion(f32[512,768]{1,0:T(8,128)S(1)} %fusion.37, s32[224]{0:T(256)S(1)} %bitcast.84), kind=kOutput, calls=%fused_computation.19 | convolution fusion | flops 1057079296 | bytes 2261888 | tf_op jit(solution)/shard_map/dot_general | solution.py:109
  32.1 5.7 %collective-permute-start.9 = (f32[1,2,8,6,128]{4,2,3,1,0:T(8,128)S(1)}, f32[1,2,8,6,128]{4,2,3,1,0:T(8,128)S(1)}, u32[]{:S(2)}, u32[]{:S(2)}) collective-permute-start(f32[1,2,8,6,128]{4,2,3,1,0:T(8,128)S(1)} %get-tuple-element.12), channel_id=1, source_target_pairs={{0,4},{4,8},{8,12},{12,16},{16,20},{20,24},{24,28},{28,32},{32,36}... | collective-permute-start | bytes 147464 | tf_op jit(solution)/shard_map/ppermute | solution.py:30
  37.9 1.9 %collective-permute-start.10 = (f32[1,2,8,6,128]{4,2,3,1,0:T(8,128)S(1)}, f32[1,2,8,6,128]{4,2,3,1,0:T(8,128)S(1)}, u32[]{:S(2)}, u32[]{:S(2)}) collective-permute-start(f32[1,2,8,6,128]{4,2,3,1,0:T(8,128)S(1)} %get-tuple-element.13), channel_id=1, source_target_pairs={{4,0},{8,4},{12,8},{16,12},{20,16},{24,20},{28,24},{32,28},{36,32}... | collective-permute-start | bytes 147464 | tf_op jit(solution)/shard_map/ppermute | solution.py:33
  39.8 6.8 %collective-permute-done.10 = f32[1,2,8,6,128]{4,2,3,1,0:T(8,128)S(1)} collective-permute-done((f32[1,2,8,6,128]{4,2,3,1,0:T(8,128)S(1)}, f32[1,2,8,6,128]{4,2,3,1,0:T(8,128)S(1)}, u32[]{:S(2)}, u32[]{:S(2)}) %collective-permute-start.10) | collective-permute-done | bytes 49184 | tf_op jit(solution)/shard_map/ppermute | solution.py:33
  46.7 2.8 %collective-permute-start.11 = (f32[4,1,8,6,128]{4,2,3,1,0:T(8,128)S(1)}, f32[4,1,8,6,128]{4,2,3,1,0:T(8,128)S(1)}, u32[]{:S(2)}, u32[]{:S(2)}) collective-permute-start(f32[4,1,8,6,128]{4,2,3,1,0:T(8,128)S(1)} %get-tuple-element.14), channel_id=1, source_target_pairs={{0,1},{1,2},{2,3},{4,5},{5,6},{6,7},{8,9},{9,10},{10,11},{12,13},{... | collective-permute-start | bytes 294920 | tf_op jit(solution)/shard_map/ppermute | solution.py:30
  49.5 2.8 %collective-permute-start.12 = (f32[4,1,8,6,128]{4,2,3,1,0:T(8,128)S(1)}, f32[4,1,8,6,128]{4,2,3,1,0:T(8,128)S(1)}, u32[]{:S(2)}, u32[]{:S(2)}) collective-permute-start(f32[4,1,8,6,128]{4,2,3,1,0:T(8,128)S(1)} %get-tuple-element.15), channel_id=1, source_target_pairs={{1,0},{2,1},{3,2},{5,4},{6,5},{7,6},{9,8},{10,9},{11,10},{13,12},{... | collective-permute-start | bytes 294920 | tf_op jit(solution)/shard_map/ppermute | solution.py:33
  52.3 2.5 %collective-permute-done.12 = f32[4,1,8,6,128]{4,2,3,1,0:T(8,128)S(1)} collective-permute-done((f32[4,1,8,6,128]{4,2,3,1,0:T(8,128)S(1)}, f32[4,1,8,6,128]{4,2,3,1,0:T(8,128)S(1)}, u32[]{:S(2)}, u32[]{:S(2)}) %collective-permute-start.12) | collective-permute-done | bytes 98336 | tf_op jit(solution)/shard_map/ppermute | solution.py:33
  54.9 0.7 fusion.35
  55.7 1.6 %slice.85 = f32[1,32,6,128]{3,2,1,0:T(8,128)} reshape(f32[32,768]{1,0:T(8,128)} %get-tuple-element.9) | data formatting | bytes 196608 | tf_op jit(solution)/shard_map/slice | solution.py:31
  57.2 0.7 slice.87
  57.9 2.7 %collective-permute-start.8 = (f32[1,32,6,128]{3,2,1,0:T(8,128)}, f32[1,32,6,128]{3,2,1,0:T(8,128)S(1)}, u32[]{:S(2)}, u32[]{:S(2)}) collective-permute-start(f32[1,32,6,128]{3,2,1,0:T(8,128)} %slice.87), channel_id=1, source_target_pairs={{1,0},{2,1},{3,2},{5,4},{6,5},{7,6},{9,8},{10,9},{11,10},{13,12},{... | collective-permute-start | bytes 294920 | tf_op jit(solution)/shard_map/ppermute | solution.py:33
  60.6 2.5 %collective-permute-start.7 = (f32[1,32,6,128]{3,2,1,0:T(8,128)}, f32[1,32,6,128]{3,2,1,0:T(8,128)S(1)}, u32[]{:S(2)}, u32[]{:S(2)}) collective-permute-start(f32[1,32,6,128]{3,2,1,0:T(8,128)} %slice.85), channel_id=1, source_target_pairs={{0,1},{1,2},{2,3},{4,5},{5,6},{6,7},{8,9},{9,10},{10,11},{12,13},{... | collective-permute-start | bytes 294920 | tf_op jit(solution)/shard_map/ppermute | solution.py:30
  63.3 0.5 collective-permute-done.8
  63.8 2.8 %collective-permute-done.7 = f32[1,32,6,128]{3,2,1,0:T(8,128)S(1)} collective-permute-done((f32[1,32,6,128]{3,2,1,0:T(8,128)}, f32[1,32,6,128]{3,2,1,0:T(8,128)S(1)}, u32[]{:S(2)}, u32[]{:S(2)}) %collective-permute-start.7) | collective-permute-done | bytes 98336 | tf_op jit(solution)/shard_map/ppermute | solution.py:30
  66.6 0.9 fusion.34
  67.4 1.7 %slice.80 = f32[1,64,6,128]{3,2,1,0:T(8,128)} reshape(f32[64,768]{1,0:T(8,128)} %get-tuple-element.6) | data formatting | bytes 393216 | tf_op jit(solution)/shard_map/slice | solution.py:31
  69.1 1.7 %slice.82 = f32[1,64,6,128]{3,2,1,0:T(8,128)} reshape(f32[64,768]{1,0:T(8,128)} %get-tuple-element.8) | data formatting | bytes 393216 | tf_op jit(solution)/shard_map/slice | solution.py:33
  70.7 1.9 %collective-permute-start.6 = (f32[1,64,6,128]{3,2,1,0:T(8,128)}, f32[1,64,6,128]{3,2,1,0:T(8,128)}, u32[]{:S(2)}, u32[]{:S(2)}) collective-permute-start(f32[1,64,6,128]{3,2,1,0:T(8,128)} %slice.82), channel_id=1, source_target_pairs={{4,0},{8,4},{12,8},{16,12},{20,16},{24,20},{28,24},{32,28},{36,32}... | collective-permute-start | bytes 589832 | tf_op jit(solution)/shard_map/ppermute | solution.py:33
  72.7 7.1 %collective-permute-start.5 = (f32[1,64,6,128]{3,2,1,0:T(8,128)}, f32[1,64,6,128]{3,2,1,0:T(8,128)}, u32[]{:S(2)}, u32[]{:S(2)}) collective-permute-start(f32[1,64,6,128]{3,2,1,0:T(8,128)} %slice.80), channel_id=1, source_target_pairs={{0,4},{4,8},{8,12},{12,16},{16,20},{20,24},{24,28},{28,32},{32,36}... | collective-permute-start | bytes 589832 | tf_op jit(solution)/shard_map/ppermute | solution.py:30
  79.8 2.1 %reshape_reshape.3 = bf16[512,3,128]{2,1,0:T(4,128)(2,1)} reshape(bf16[4,384,128]{2,1,0:T(8,128)(2,1)} %copy-done.1) | data formatting | bytes 786432 | tf_op jit(solution)/shard_map/reshape;reshape | solution.py:143
  81.9 1.6 %copy.39 = f32[512,768]{0,1:T(8,128)} copy(f32[512,768]{1,0:T(8,128)S(1)} %fusion.37) | data formatting | bytes 3145728 | tf_op jit(solution)/shard_map/dot_general | solution.py:104
  83.5 1.8 %copy.41 = bf16[512,3,128]{2,0,1:T(8,128)(2,1)} copy(bf16[512,3,128]{2,1,0:T(4,128)(2,1)} %reshape_reshape.3) | data formatting | bytes 786432
  85.4 1.9 %copy.40 = f32[512,6,128]{2,0,1:T(8,128)S(1)} copy(f32[512,6,128]{0,2,1:T(8,128)} %bitcast.74) | data formatting | bytes 3145728 | tf_op jit(solution)/shard_map/reshape | solution.py:106
  87.3 1.1 %pad_maximum_fusion = f32[2,64,6,128]{3,2,1,0:T(8,128)S(1)} fusion(f32[1,64,6,128]{3,2,1,0:T(8,128)} %collective-permute-done.6, f32[1,64,6,128]{3,2,1,0:T(8,128)} %collective-permute-done.5), kind=kLoop, calls=%fused_computation.15 | loop fusion | flops 98304 | bytes 786432 | tf_op jit(solution)/shard_map/stack | solution.py:115
  88.6 1.2 %copy.37 = f32[768,224]{1,0:T(8,128)} copy(f32[768,224]{0,1:T(8,128)S(1)} %maximum_bitcast_fusion) | data formatting | bytes 1376256 | tf_op jit(solution)/shard_map/dot_general | solution.py:137
  89.8 3.2 %divide_convert_fusion = bf16[512,6,128]{2,0,1:T(8,128)(2,1)} fusion(f32[512,6,128]{2,0,1:T(8,128)S(1)} %copy.40, f32[6,128,224]{2,1,0:T(8,128)} %bitcast.78, f32[512]{0:T(512)S(1)} %copy-done.7, pred[512]{0:T(512)(128)(4,1)S(1)} %broadcast_compare_fusion, s32[224]{0:T(256)S(1)} %bitcast.86), kind=kOutput, calls=%fused_computation.5 | convolution fusion | flops 1058373632 | bytes 3050880 | tf_op jit(solution)/shard_map/dot_general | solution.py:137
  (59 shorter events, 1.7 us)
Async XLA Ops:
  0.6 20.8 %copy-start = (bf16[4,384,384]{2,1,0:T(8,128)(2,1)S(1)}, bf16[4,384,384]{2,1,0:T(8,128)(2,1)}, u32[]{:S(2)}) copy-start(bf16[4,384,384]{2,1,0:T(8,128)(2,1)} %param.15) | copy-start | bytes 3538948
  0.6 3.8 %collective-permute-start = (f32[24,128]{1,0:T(8,128)}, f32[24,128]{1,0:T(8,128)S(1)}, u32[]{:S(2)}, u32[]{:S(2)}) collective-permute-start(f32[24,128]{1,0:T(8,128)} %param.11), channel_id=1, source_target_pairs={{0,1},{1,2},{2,3},{3,0},{4,5},{5,6},{6,7},{7,4},{8,9},{9,10},{10,1... | collective-permute-start | bytes 36872 | tf_op jit(solution)/shard_map/ppermute | solution.py:18
  1.9 6.1 %collective-permute-start.2 = (f32[24,128]{1,0:T(8,128)}, f32[24,128]{1,0:T(8,128)S(1)}, u32[]{:S(2)}, u32[]{:S(2)}) collective-permute-start(f32[24,128]{1,0:T(8,128)} %param.11), channel_id=1, source_target_pairs={{0,3},{1,0},{2,1},{3,2},{4,7},{5,4},{6,5},{7,6},{8,11},{9,8},{10,9... | collective-permute-start | bytes 36872 | tf_op jit(solution)/shard_map/ppermute | solution.py:20
  4.5 2.8 %collective-permute-start.1 = (f32[24,128]{1,0:T(8,128)S(1)}, f32[24,128]{1,0:T(8,128)S(1)}, u32[]{:S(2)}, u32[]{:S(2)}) collective-permute-start(f32[24,128]{1,0:T(8,128)S(1)} %collective-permute-done), channel_id=1, source_target_pairs={{0,1},{1,2},{2,3},{3,0},{4,5},{5,6},{6,7},{7,4},{8,9},{9,10},{10,1... | collective-permute-start | bytes 36872 | tf_op jit(solution)/shard_map/ppermute | solution.py:18
  8.8 11.9 %collective-permute-start.4 = (f32[96,128]{1,0:T(8,128)S(1)}, f32[96,128]{1,0:T(8,128)S(1)}, u32[]{:S(2)}, u32[]{:S(2)}) collective-permute-start(f32[96,128]{1,0:T(8,128)S(1)} %constant_dynamic-slice_fusion), channel_id=1, source_target_pairs={{4,0},{8,4},{12,8},{16,12},{20,16},{24,20},{28,24},{32,28},{36,32}... | collective-permute-start | bytes 147464 | tf_op jit(solution)/shard_map/ppermute | solution.py:33
  12.8 7.9 %collective-permute-start.3 = (f32[96,128]{1,0:T(8,128)S(1)}, f32[96,128]{1,0:T(8,128)S(1)}, u32[]{:S(2)}, u32[]{:S(2)}) collective-permute-start(f32[96,128]{1,0:T(8,128)S(1)} %constant_dynamic-slice_fusion), channel_id=1, source_target_pairs={{0,4},{4,8},{8,12},{12,16},{16,20},{20,24},{24,28},{28,32},{32,36}... | collective-permute-start | bytes 147464 | tf_op jit(solution)/shard_map/ppermute | solution.py:30
  20.0 0.9 copy-start.4
  22.2 4.1 %copy-start.1 = (bf16[4,384,128]{2,1,0:T(8,128)(2,1)}, bf16[4,384,128]{2,1,0:T(8,128)(2,1)S(1)}, u32[]{:S(2)}) copy-start(bf16[4,384,128]{2,1,0:T(8,128)(2,1)S(1)} %copy.32) | copy-start | bytes 1179652
  26.3 0.7 copy-start.6
  27.7 3.4 %copy-start.5 = (s32[1,224]{1,0:T(1,128)S(1)}, s32[1,224]{1,0:T(1,128)}, u32[]{:S(2)}) copy-start(s32[1,224]{1,0:T(1,128)} %param.20) | copy-start | bytes 2692
  32.1 7.7 %collective-permute-start.9 = (f32[1,2,8,6,128]{4,2,3,1,0:T(8,128)S(1)}, f32[1,2,8,6,128]{4,2,3,1,0:T(8,128)S(1)}, u32[]{:S(2)}, u32[]{:S(2)}) collective-permute-start(f32[1,2,8,6,128]{4,2,3,1,0:T(8,128)S(1)} %get-tuple-element.12), channel_id=1, source_target_pairs={{0,4},{4,8},{8,12},{12,16},{16,20},{20,24},{24,28},{28,32},{32,36}... | collective-permute-start | bytes 147464 | tf_op jit(solution)/shard_map/ppermute | solution.py:30
  37.9 8.7 %collective-permute-start.10 = (f32[1,2,8,6,128]{4,2,3,1,0:T(8,128)S(1)}, f32[1,2,8,6,128]{4,2,3,1,0:T(8,128)S(1)}, u32[]{:S(2)}, u32[]{:S(2)}) collective-permute-start(f32[1,2,8,6,128]{4,2,3,1,0:T(8,128)S(1)} %get-tuple-element.13), channel_id=1, source_target_pairs={{4,0},{8,4},{12,8},{16,12},{20,16},{24,20},{28,24},{32,28},{36,32}... | collective-permute-start | bytes 147464 | tf_op jit(solution)/shard_map/ppermute | solution.py:33
  46.7 5.7 %collective-permute-start.11 = (f32[4,1,8,6,128]{4,2,3,1,0:T(8,128)S(1)}, f32[4,1,8,6,128]{4,2,3,1,0:T(8,128)S(1)}, u32[]{:S(2)}, u32[]{:S(2)}) collective-permute-start(f32[4,1,8,6,128]{4,2,3,1,0:T(8,128)S(1)} %get-tuple-element.14), channel_id=1, source_target_pairs={{0,1},{1,2},{2,3},{4,5},{5,6},{6,7},{8,9},{9,10},{10,11},{12,13},{... | collective-permute-start | bytes 294920 | tf_op jit(solution)/shard_map/ppermute | solution.py:30
  49.5 5.4 %collective-permute-start.12 = (f32[4,1,8,6,128]{4,2,3,1,0:T(8,128)S(1)}, f32[4,1,8,6,128]{4,2,3,1,0:T(8,128)S(1)}, u32[]{:S(2)}, u32[]{:S(2)}) collective-permute-start(f32[4,1,8,6,128]{4,2,3,1,0:T(8,128)S(1)} %get-tuple-element.15), channel_id=1, source_target_pairs={{1,0},{2,1},{3,2},{5,4},{6,5},{7,6},{9,8},{10,9},{11,10},{13,12},{... | collective-permute-start | bytes 294920 | tf_op jit(solution)/shard_map/ppermute | solution.py:33
  57.9 5.9 %collective-permute-start.8 = (f32[1,32,6,128]{3,2,1,0:T(8,128)}, f32[1,32,6,128]{3,2,1,0:T(8,128)S(1)}, u32[]{:S(2)}, u32[]{:S(2)}) collective-permute-start(f32[1,32,6,128]{3,2,1,0:T(8,128)} %slice.87), channel_id=1, source_target_pairs={{1,0},{2,1},{3,2},{5,4},{6,5},{7,6},{9,8},{10,9},{11,10},{13,12},{... | collective-permute-start | bytes 294920 | tf_op jit(solution)/shard_map/ppermute | solution.py:33
  60.6 5.9 %collective-permute-start.7 = (f32[1,32,6,128]{3,2,1,0:T(8,128)}, f32[1,32,6,128]{3,2,1,0:T(8,128)S(1)}, u32[]{:S(2)}, u32[]{:S(2)}) collective-permute-start(f32[1,32,6,128]{3,2,1,0:T(8,128)} %slice.85), channel_id=1, source_target_pairs={{0,1},{1,2},{2,3},{4,5},{5,6},{6,7},{8,9},{9,10},{10,11},{12,13},{... | collective-permute-start | bytes 294920 | tf_op jit(solution)/shard_map/ppermute | solution.py:30
  70.7 16.5 %collective-permute-start.6 = (f32[1,64,6,128]{3,2,1,0:T(8,128)}, f32[1,64,6,128]{3,2,1,0:T(8,128)}, u32[]{:S(2)}, u32[]{:S(2)}) collective-permute-start(f32[1,64,6,128]{3,2,1,0:T(8,128)} %slice.82), channel_id=1, source_target_pairs={{4,0},{8,4},{12,8},{16,12},{20,16},{24,20},{28,24},{32,28},{36,32}... | collective-permute-start | bytes 589832 | tf_op jit(solution)/shard_map/ppermute | solution.py:33
  72.7 14.6 %collective-permute-start.5 = (f32[1,64,6,128]{3,2,1,0:T(8,128)}, f32[1,64,6,128]{3,2,1,0:T(8,128)}, u32[]{:S(2)}, u32[]{:S(2)}) collective-permute-start(f32[1,64,6,128]{3,2,1,0:T(8,128)} %slice.80), channel_id=1, source_target_pairs={{0,4},{4,8},{8,12},{12,16},{16,20},{20,24},{24,28},{28,32},{32,36}... | collective-permute-start | bytes 589832 | tf_op jit(solution)/shard_map/ppermute | solution.py:30
  87.3 1.3 %copy-start.2 = (f32[64,768]{1,0:T(8,128)S(1)}, f32[64,768]{1,0:T(8,128)}, u32[]{:S(2)}) copy-start(f32[64,768]{1,0:T(8,128)} %get-tuple-element.7) | copy-start | bytes 589828
  87.3 1.3 %copy-start.3 = (f32[32,768]{1,0:T(8,128)S(1)}, f32[32,768]{1,0:T(8,128)}, u32[]{:S(2)}) copy-start(f32[32,768]{1,0:T(8,128)} %get-tuple-element.10) | copy-start | bytes 294916
  88.5 1.3 %copy-start.7 = (f32[512]{0:T(512)S(1)}, f32[512]{0:T(512)}, u32[]{:S(2)}) copy-start(f32[512]{0:T(512)} %param.21) | copy-start | bytes 6148
